TPU v7x, 256 devices: a whole 4x4x8 slice. The times are simulated.
256 devices in a mesh: seq: 64 (over y, x, z_hi, core), chan: 4 (over z_lo).
Axes of the slice: x: 4, y: 4, z: 8 (z_hi: 2, z_lo: 4; z = z_hi * 4 + z_lo), core: 2. Of those that a mesh axis runs over, the one named last changes fastest.
Arguments:
- tokens: bfloat16 [512, 768, 1024], P('seq', 'chan'), may hold values from -24 to 24, as said below
- filter_gain: bfloat16 [512, 768, 1024], P('seq', 'chan'), may hold values from -4 to 4
- row_factor: bfloat16 [1024, 1024], replicated, may hold values from -0.1875 to 0.1875
- col_factor: bfloat16 [512, 512], replicated, may hold values from -0.25 to 0.25
- up_weight: bfloat16 [4, 192, 768], P('chan'), may hold values from -0.4375 to 0.4375
- down_weight: bfloat16 [4, 192, 768], P('chan'), may hold values from -0.21875 to 0.21875
Outputs:
- layer_out: bfloat16 [512, 768, 1024], P('seq', 'chan')
Inputs may be any that keep to these rules, and one draw needn't show every extreme that they name: `tokens`: layer activations.
All inputs are finite; a program needn't handle non-finite values.
Results may differ from a plain program's by a relative error of at most 0.0075.
Values may be sent and summed in bfloat16 or wider, within the bound.
A program may use at most 128 MiB of HBM per device.

v0:
```python
import jax
import jax.numpy as jnp
from jax import lax
from jax.sharding import PartitionSpec as P

D = 768


def column_mix(received, col_factor, groups):
    local_rows, channels, columns = received.shape
    narrow = columns // groups
    blocks = received.reshape(local_rows, channels, groups, narrow)
    factor = col_factor.reshape(groups, local_rows, groups, local_rows)
    mixed = jnp.einsum("stqr,rcqj->tcsj", factor, blocks, preferred_element_type=jnp.float32)
    return mixed.astype(jnp.bfloat16).reshape(local_rows, channels, columns)


def finish(source, mixed, up_weight, down_weight):
    src = source.astype(jnp.float32)
    gated = src + mixed.astype(jnp.float32) * jax.nn.sigmoid(src)
    total = lax.psum(jnp.sum(gated, axis=1).astype(jnp.bfloat16), "chan").astype(jnp.float32)
    mean = total / D
    centered = gated - mean[:, None, :]
    spread = lax.psum(jnp.sum(centered * centered, axis=1), "chan") / D
    normed = (centered * lax.rsqrt(spread + 1e-05)[:, None, :]).astype(jnp.bfloat16)
    nblocks = up_weight.shape[0]
    block_width = up_weight.shape[1]
    flat = normed.reshape(gated.shape[0], nblocks, block_width, gated.shape[2])
    hidden = jax.nn.gelu(
        jnp.einsum("xnky,nkh->xnhy", flat, up_weight, preferred_element_type=jnp.float32)
    ).astype(jnp.bfloat16)
    back = jnp.einsum("xnhy,nkh->xnky", hidden, down_weight, preferred_element_type=jnp.float32)
    return (gated + back.reshape(gated.shape)).astype(jnp.bfloat16)


def body(tokens, filter_gain, row_factor, col_factor, up_weight, down_weight):
    groups = lax.axis_size("seq")
    spun = jnp.einsum("rck,bk->rcb", tokens, row_factor, preferred_element_type=jnp.float32)
    filtered = (filter_gain.astype(jnp.float32) * spun).astype(jnp.bfloat16)
    col_filtered, col_source = (
        lax.all_to_all(filtered, "seq", split_axis=2, concat_axis=2, tiled=True),
        lax.all_to_all(tokens, "seq", split_axis=2, concat_axis=2, tiled=True),
    )
    mixed = column_mix(col_filtered, col_factor, groups)
    result = finish(col_source, mixed, up_weight, down_weight)
    return lax.all_to_all(result, "seq", split_axis=2, concat_axis=2, tiled=True)


def solution(mesh):
    return jax.shard_map(
        body,
        mesh=mesh,
        in_specs=(
            P("seq", "chan", None),
            P("seq", "chan", None),
            P(),
            P(),
            P("chan", None, None),
            P("chan", None, None),
        ),
        out_specs=P("seq", "chan", None),
        check_vma=False,
    )
```

profile of v0, /device:TPU:1, one launch (start us, length us, event | category | flops | bytes accessed | tf_op | source)
XLA Modules:
  0.0 421.7 jit_solution(13764401925225365308)
XLA Ops:
  0.0 0.0 copy-start
  0.0 1.6 copy-done
  1.6 7.2 %multiply_convert_fusion.1 = bf16[8,192,1024]{2,1,0:T(8,128)(2,1)} fusion(bf16[8,192,1024]{2,1,0:T(8,128)(2,1)} %param.7, bf16[8,192,1024]{2,1,0:T(8,128)(2,1)} %param.6, bf16[1024,1024]{1,0:T(8,128)(2,1)S(1)} %copy-done), kind=kOutput, calls=%fused_computation.24 | convolution fusion | flops 3225944064 | bytes 11534336 | tf_op jit(solution)/shard_map/rck,bk->rcb/dot_general | solution.py:38
  8.8 6.8 %copy.18 = bf16[8,192,1024]{1,0,2:T(8,128)(2,1)} copy(bf16[8,192,1024]{2,1,0:T(8,128)(2,1)} %multiply_convert_fusion.1) | data formatting | bytes 6291456 | tf_op jit(solution)/shard_map/convert_element_type | solution.py:39
  15.6 15.8 %all-to-all-start.1 = ((bf16[8,192,1024]{1,0,2:T(8,128)(2,1)}), bf16[8,192,1024]{1,0,2:T(8,128)(2,1)}, u32[]{:S(2)}, u32[]{:S(2)}) async-start(bf16[8,192,1024]{1,0,2:T(8,128)(2,1)} %copy.18), calls=%async_computation.1 | async-start | bytes 8388608 | tf_op jit(solution)/shard_map/all_to_all | solution.py:41
  31.4 0.0 copy-start.2
  31.4 7.0 %copy.16 = bf16[8,192,1024]{1,0,2:T(8,128)(2,1)} copy(bf16[8,192,1024]{2,1,0:T(8,128)(2,1)} %param.6) | data formatting | bytes 6291456 | tf_op args[0]
  38.4 93.8 %all-to-all-done.1 = bf16[8,192,1024]{1,0,2:T(8,128)(2,1)} async-done(((bf16[8,192,1024]{1,0,2:T(8,128)(2,1)}), bf16[8,192,1024]{1,0,2:T(8,128)(2,1)}, u32[]{:S(2)}, u32[]{:S(2)}) %all-to-all-start.1) | async-done | bytes 3145760 | tf_op jit(solution)/shard_map/all_to_all | solution.py:41
  132.3 5.4 %all-to-all-start = ((bf16[8,192,1024]{1,0,2:T(8,128)(2,1)}), bf16[8,192,1024]{1,0,2:T(8,128)(2,1)}, u32[]{:S(2)}, u32[]{:S(2)}) async-start(bf16[8,192,1024]{1,0,2:T(8,128)(2,1)} %copy.16), calls=%async_computation | async-start | bytes 8388608 | tf_op jit(solution)/shard_map/all_to_all | solution.py:42
  137.7 0.0 copy-done.2
  137.7 10.8 %reshape.29 = bf16[64,8,64,8]{3,2,1,0:T(8,128)(2,1)} reshape(bf16[512,512]{1,0:T(8,128)(2,1)S(1)} %copy-done.2) | data formatting | bytes 1048576 | tf_op jit(solution)/shard_map/reshape | solution.py:13
  148.5 7.2 %copy.21 = bf16[64,8,64,8]{2,0,3,1:T(8,128)(2,1)S(1)} copy(bf16[64,8,64,8]{3,2,1,0:T(8,128)(2,1)} %reshape.29) | data formatting | bytes 1048576 | tf_op jit(solution)/shard_map/reshape | solution.py:13
  155.7 8.5 %convert_bitcast_fusion = f32[8,192,64,16]{1,2,0,3:T(8,128)S(1)} fusion(bf16[8,192,64,16,1]{1,0,3,2,4:T(8,128)(2,1)} %bitcast.2, bf16[64,8,64,8]{2,0,3,1:T(8,128)(2,1)S(1)} %copy.21), kind=kOutput, calls=%fused_computation.12 | convolution fusion | flops 1613758464 | bytes 9961472 | tf_op jit(solution)/shard_map/stqr,rcqj->tcsj/dot_general | solution.py:14
  164.2 8.0 %copy.22 = f32[8,192,64,16]{1,3,2,0:T(8,128)} copy(f32[8,192,64,16]{1,2,0,3:T(8,128)S(1)} %convert_bitcast_fusion) | data formatting | bytes 12582912 | tf_op jit(solution)/shard_map/convert_element_type | solution.py:20
  172.2 8.5 %copy.23 = f32[8,192,1024]{2,1,0:T(8,128)} copy(f32[8,192,1024]{1,2,0:T(8,128)} %bitcast.53) | data formatting | bytes 12582912 | tf_op jit(solution)/shard_map/convert_element_type | solution.py:20
  180.6 11.6 %all-to-all-done = bf16[8,192,1024]{1,0,2:T(8,128)(2,1)} async-done(((bf16[8,192,1024]{1,0,2:T(8,128)(2,1)}), bf16[8,192,1024]{1,0,2:T(8,128)(2,1)}, u32[]{:S(2)}, u32[]{:S(2)}) %all-to-all-start) | async-done | bytes 3145760 | tf_op jit(solution)/shard_map/all_to_all | solution.py:42
  192.2 6.4 %copy.17 = bf16[8,192,1024]{2,1,0:T(8,128)(2,1)} copy(bf16[8,192,1024]{1,0,2:T(8,128)(2,1)} %all-to-all-done) | data formatting | bytes 6291456 | tf_op jit(solution)/shard_map/all_to_all | solution.py:42
  198.6 6.4 %fusion.37 = (bf16[8,1024]{1,0:T(8,128)(2,1)S(1)}, f32[8,192,1024]{2,1,0:T(8,128)}) fusion(f32[8,192,1024]{2,1,0:T(8,128)} %copy.23, bf16[8,192,1024]{2,1,0:T(8,128)(2,1)} %copy.17), kind=kLoop, calls=%fused_computation.39 | loop fusion | flops 11001856 | bytes 15745024 | tf_op jit(solution)/shard_map/reduce_sum | solution.py:21
  205.0 0.0 copy-start.3
  205.0 0.0 copy-start.4
  205.0 59.2 %psum.14 = bf16[8,1024]{1,0:T(8,128)(2,1)S(1)} all-reduce(bf16[8,1024]{1,0:T(8,128)(2,1)S(1)} %get-tuple-element.5), channel_id=1, replica_groups=mesh['seq'=64,'chan'=4] {'chan'}, use_global_device_ids=true, to_apply=%region_1.0 | all-reduce | flops 8192 | bytes 32768 | tf_op jit(solution)/shard_map/psum | solution.py:21
  264.2 3.6 multiply_reduce_fusion
  267.9 12.3 %psum.15 = f32[8,1024]{1,0:T(8,128)S(1)} all-reduce(f32[8,1024]{1,0:T(8,128)S(1)} %multiply_reduce_fusion), channel_id=1, replica_groups=mesh['seq'=64,'chan'=4] {'chan'}, use_global_device_ids=true, to_apply=%region_3.0 | all-reduce | flops 8192 | bytes 65536 | tf_op jit(solution)/shard_map/psum | solution.py:24
  280.2 0.0 copy-done.3
  280.2 0.0 copy-done.4
  280.2 14.8 %fusion.17 = bf16[8,192,1024]{2,1,0:T(8,128)(2,1)} fusion(f32[8,192,1024]{2,1,0:T(8,128)} %get-tuple-element.6, f32[8,1024]{1,0:T(8,128)S(1)} %add_rsqrt_fusion, f32[8,1024]{1,0:T(8,128)S(1)} %convert_multiply_fusion, bf16[1,192,768]{2,1,0:T(8,128)(2,1)S(1)} %copy-done.3, bf16[1,192,768]{2,1,0:T(8,128)(2,1)S(1)} %copy-done.4), kind=kOutput, calls=%fused_computation.21 | convolution fusion | flops 4896325632 | bytes 10092544 | tf_op jit(solution)/shard_map/xnhy,nkh->xnky/dot_general | solution.py:32
  295.0 0.0 copy-start.1
  295.0 6.9 %copy.25 = bf16[8,192,1024]{1,0,2:T(8,128)(2,1)} copy(bf16[8,192,1024]{2,1,0:T(8,128)(2,1)} %fusion.17) | data formatting | bytes 6291456 | tf_op jit(solution)/shard_map/convert_element_type | solution.py:33
  302.0 113.4 %all_to_all.15 = bf16[8,192,1024]{1,0,2:T(8,128)(2,1)} all-to-all(bf16[8,192,1024]{1,0,2:T(8,128)(2,1)} %copy.25), channel_id=1, replica_groups=mesh['seq'=64,'chan'=4] {'seq'}, dimensions={2} | all-to-all | bytes 6291456 | tf_op jit(solution)/shard_map/all_to_all | solution.py:46
  415.4 6.4 %copy.26 = bf16[8,192,1024]{2,1,0:T(8,128)(2,1)} copy(bf16[8,192,1024]{1,0,2:T(8,128)(2,1)} %all_to_all.15) | data formatting | bytes 6291456 | tf_op jit(solution)/shard_map/all_to_all | solution.py:46
  421.7 0.0 copy-done.1
  (2 shorter events, 0.0 us)
Async XLA Ops:
  0.0 1.6 copy-start
  15.6 116.6 %all-to-all-start.1 = ((bf16[8,192,1024]{1,0,2:T(8,128)(2,1)}), bf16[8,192,1024]{1,0,2:T(8,128)(2,1)}, u32[]{:S(2)}, u32[]{:S(2)}) async-start(bf16[8,192,1024]{1,0,2:T(8,128)(2,1)} %copy.18), calls=%async_computation.1 | async-start | bytes 8388608 | tf_op jit(solution)/shard_map/all_to_all | solution.py:41
  31.4 106.3 %copy-start.2 = (bf16[512,512]{1,0:T(8,128)(2,1)S(1)}, bf16[512,512]{1,0:T(8,128)(2,1)}, u32[]{:S(2)}) copy-start(bf16[512,512]{1,0:T(8,128)(2,1)} %param.9) | copy-start | bytes 1572868
  132.3 60.0 %all-to-all-start = ((bf16[8,192,1024]{1,0,2:T(8,128)(2,1)}), bf16[8,192,1024]{1,0,2:T(8,128)(2,1)}, u32[]{:S(2)}, u32[]{:S(2)}) async-start(bf16[8,192,1024]{1,0,2:T(8,128)(2,1)} %copy.16), calls=%async_computation | async-start | bytes 8388608 | tf_op jit(solution)/shard_map/all_to_all | solution.py:42
  205.0 75.2 %copy-start.3 = (bf16[1,192,768]{2,1,0:T(8,128)(2,1)S(1)}, bf16[1,192,768]{2,1,0:T(8,128)(2,1)}, u32[]{:S(2)}) copy-start(bf16[1,192,768]{2,1,0:T(8,128)(2,1)} %param.11) | copy-start | bytes 884740
  205.0 75.2 %copy-start.4 = (bf16[1,192,768]{2,1,0:T(8,128)(2,1)S(1)}, bf16[1,192,768]{2,1,0:T(8,128)(2,1)}, u32[]{:S(2)}) copy-start(bf16[1,192,768]{2,1,0:T(8,128)(2,1)} %param.10) | copy-start | bytes 884740
  295.0 126.7 %copy-start.1 = (bf16[1024,1024]{1,0:T(8,128)(2,1)S(1)}, bf16[1024,1024]{1,0:T(8,128)(2,1)}, u32[]{:S(2)}) copy-start(bf16[1024,1024]{1,0:T(8,128)(2,1)} %param.8) | copy-start | bytes 6291460
where the time goes:
time: 423 us; the launch traced here: 422 us
  blocking collectives  185 us (44%)
  waiting for transfers between devices  105 us (25%)
  local copies, waits for them, and re-layouts  69.5 us (16%)
  matrix products  30.6 us (7%)
  starting transfers between devices  21.2 us (5%)
  other arithmetic  10.1 us (2%)
    all_to_all x1, blocking collectives, body(): lax.all_to_all(result, 'seq', split_axis=2, concat_axis=2, tiled=True)  113 us
    all_to_all x1, waiting for transfers between devices, body(): lax.all_to_all(filtered, 'seq', split_axis=2, concat_axis=2, tiled=True)  93.8 us
    psum x1, blocking collectives, finish(): lax.psum(jnp.sum(gated, axis=1).astype(jnp.bfloat16), 'chan')  59.2 us
    reshape x2, local copies, waits for them, and re-layouts, column_mix(): factor = col_factor.reshape(groups, local_rows, groups, local_rows)  18 us
    convert_element_type x2, local copies, waits for them, and re-layouts, finish(): gated = src + mixed.astype(jnp.float32) * jax.nn.sigmoid(src)  16.4 us
    all_to_all x1, starting transfers between devices, body(): lax.all_to_all(filtered, 'seq', split_axis=2, concat_axis=2, tiled=True)  15.8 us
    dot_general x1, matrix products, finish(): jnp.einsum('xnhy,nkh->xnky', hidden, down_weight, preferred_element_type=...  14.8 us
    psum x1, blocking collectives, finish(): spread = lax.psum(jnp.sum(centered * centered, axis=1), 'chan') / D  12.3 us
  transfers between devices with their start and end apart: 2, of which 2 were waited for; matrix products, arithmetic and copies ran while one was open for 12% of the time, Pallas kernels for 0%

commit v1 on v0

v1 whole, which is shorter than its diff:
```python
import jax
import jax.numpy as jnp
from jax import lax
from jax.sharding import PartitionSpec as P

D = 768


def finish(source, mixed, up_weight, down_weight):
    src = source.astype(jnp.float32)
    gated = src + mixed.astype(jnp.float32) * jax.nn.sigmoid(src)
    total = lax.psum(jnp.sum(gated, axis=1), "chan")
    mean = total / D
    centered = gated - mean[:, None, :]
    spread = lax.psum(jnp.sum(centered * centered, axis=1), "chan") / D
    normed = (centered * lax.rsqrt(spread + 1e-05)[:, None, :]).astype(jnp.bfloat16)
    hidden = jax.nn.gelu(
        jnp.einsum("xky,kh->xhy", normed, up_weight[0], preferred_element_type=jnp.float32)
    ).astype(jnp.bfloat16)
    back = jnp.einsum("xhy,kh->xky", hidden, down_weight[0], preferred_element_type=jnp.float32)
    return (gated + back).astype(jnp.bfloat16)


def body(tokens, filter_gain, row_factor, col_factor, up_weight, down_weight):
    spun = jnp.einsum("rck,bk->rcb", tokens, row_factor, preferred_element_type=jnp.float32)
    filtered = (filter_gain.astype(jnp.float32) * spun).astype(jnp.bfloat16)
    by_channel = jnp.transpose(filtered, (1, 0, 2))
    owned = lax.all_to_all(by_channel, "seq", split_axis=0, concat_axis=1, tiled=True)
    mixed = jnp.einsum("ak,ckb->cab", col_factor, owned, preferred_element_type=jnp.float32)
    back = lax.all_to_all(mixed.astype(jnp.bfloat16), "seq", split_axis=1, concat_axis=0, tiled=True)
    return finish(tokens, jnp.transpose(back, (1, 0, 2)), up_weight, down_weight)


def solution(mesh):
    return jax.shard_map(
        body,
        mesh=mesh,
        in_specs=(
            P("seq", "chan", None),
            P("seq", "chan", None),
            P(),
            P(),
            P("chan", None, None),
            P("chan", None, None),
        ),
        out_specs=P("seq", "chan", None),
        check_vma=False,
    )
```

time: 423 us -> 281 us (0.66)
  waiting for transfers between devices: 105 us -> 0 us
  local copies, waits for them, and re-layouts: 69.5 us -> 13 us
  blocking collectives: 185 us -> 225 us
  starting transfers between devices: 21.2 us -> 0 us
  matrix products: 30.6 us -> 24.4 us
    all_to_all x2 -> x0, waiting for transfers between devices: 105 us -> none  [the longest x1 93.8 us: body(): lax.all_to_all(filtered, 'seq', split_axis=2, concat_axis=2, tiled=True)]
    all_to_all x1 -> x2, blocking collectives: 113 us -> 199 us  [the longest x1 106 us: body(): lax.all_to_all(mixed.astype(jnp.bfloat16), 'seq', split_axis=1, concat_ax...]
    psum x1, blocking collectives: 59.2 us -> 13.9 us  [finish(): total = lax.psum(jnp.sum(gated, axis=1), 'chan')]
    all_to_all x2 -> x0, starting transfers between devices: 21.2 us -> none  [the longest x1 15.8 us: body(): lax.all_to_all(filtered, 'seq', split_axis=2, concat_axis=2, tiled=True)]
    reshape x2 -> x0, local copies, waits for them, and re-layouts: 18 us -> none  [column_mix(): factor = col_factor.reshape(groups, local_rows, groups, local_rows)]
    convert_element_type x2 -> x1, local copies, waits for them, and re-layouts: 16.4 us -> 1.11 us  [finish(): gated = src + mixed.astype(jnp.float32) * jax.nn.sigmoid(src)]
    all_to_all x2 -> x0, local copies, waits for them, and re-layouts: 12.7 us -> none  [the longest x1 6.36 us: body(): lax.all_to_all(tokens, 'seq', split_axis=2, concat_axis=2, tiled=True)]
    unnamed x11 -> x10, local copies, waits for them, and re-layouts: 8.6 us -> 2.37 us
  transfers between devices with their start and end apart: 2 -> 0, of which waited for: 2 -> 0; matrix products, arithmetic and copies ran while one was open for 12% -> 0% of each run, Pallas kernels for 0% -> 0%
where the time goes in v1:
time: 281 us; the launch traced here: 276 us
  blocking collectives  225 us (80%)
  matrix products  24.4 us (9%)
  other arithmetic  13.3 us (5%)
  local copies, waits for them, and re-layouts  13 us (5%)
    all_to_all x1, blocking collectives, body(): lax.all_to_all(mixed.astype(jnp.bfloat16), 'seq', split_axis=1, concat_ax...  106 us
    all_to_all x1, blocking collectives, body(): lax.all_to_all(by_channel, 'seq', split_axis=0, concat_axis=1, tiled=True)  93.2 us
    dot_general x1, matrix products, finish(): jnp.einsum('xhy,kh->xky', hidden, down_weight[0], preferred_element_type=...  14.8 us
    psum x1, blocking collectives, finish(): total = lax.psum(jnp.sum(gated, axis=1), 'chan')  13.9 us
    psum x1, blocking collectives, finish(): spread = lax.psum(jnp.sum(centered * centered, axis=1), 'chan') / D  12.5 us
    reduce_sum x1, other arithmetic, finish(): total = lax.psum(jnp.sum(gated, axis=1), 'chan')  8.29 us
    convert_element_type x1, local copies, waits for them, and re-layouts, body(): mixed.astype(jnp.bfloat16)  7.78 us
    dot_general x1, matrix products, body(): jnp.einsum('rck,bk->rcb', tokens, row_factor, preferred_element_type=jnp....  6.08 us

profile of v1, /device:TPU:1, one launch (start us, length us, event | category | flops | bytes accessed | tf_op | source)
XLA Modules:
  0.0 276.0 jit_solution(5488151017067106785)
XLA Ops:
  0.0 0.0 copy-start
  0.0 1.6 copy-done
  1.6 6.1 %fusion.17 = bf16[192,8,1024]{2,0,1:T(8,128)(2,1)S(1)} fusion(bf16[8,192,1024]{2,1,0:T(8,128)(2,1)} %param.7, bf16[8,192,1024]{2,1,0:T(8,128)(2,1)} %param.6, bf16[1024,1024]{1,0:T(8,128)(2,1)S(1)} %copy-done), kind=kOutput, calls=%fused_computation.23 | convolution fusion | flops 3225944064 | bytes 11534336 | tf_op jit(solution)/shard_map/rck,bk->rcb/dot_general | solution.py:25
  7.7 0.0 copy-start.2
  7.7 1.7 copy.17
  9.4 93.2 %all_to_all.27 = bf16[192,8,1024]{2,1,0:T(8,128)(2,1)S(1)} all-to-all(bf16[192,8,1024]{2,1,0:T(8,128)(2,1)S(1)} %copy.17), channel_id=1, replica_groups=mesh['seq'=64,'chan'=4] {'seq'}, dimensions={0} | all-to-all | bytes 6291456 | tf_op jit(solution)/shard_map/all_to_all | solution.py:28
  102.7 0.0 copy-done.2
  102.7 3.5 %convert_bitcast_fusion.1 = bf16[3,512,1024]{1,2,0:T(8,128)(2,1)} fusion(bf16[3,64,8,1024]{3,2,0,1:T(8,128)(2,1)S(1)} %bitcast.47, bf16[512,512]{1,0:T(8,128)(2,1)S(1)} %copy-done.2), kind=kOutput, calls=%fused_computation.29 | convolution fusion | flops 1612185600 | bytes 6815744 | tf_op jit(solution)/shard_map/ak,ckb->cab/dot_general | solution.py:29
  106.2 7.8 %copy.20 = bf16[3,512,1024]{2,0,1:T(4,128)(2,1)} copy(bf16[3,512,1024]{1,2,0:T(8,128)(2,1)} %convert_bitcast_fusion.1) | data formatting | bytes 6291456 | tf_op jit(solution)/shard_map/convert_element_type | solution.py:30
  114.0 105.5 %all_to_all.28 = bf16[3,512,1024]{2,0,1:T(4,128)(2,1)S(1)} all-to-all(bf16[3,512,1024]{2,0,1:T(4,128)(2,1)} %copy.20), channel_id=1, replica_groups=mesh['seq'=64,'chan'=4] {'seq'}, dimensions={1} | all-to-all | bytes 6291456 | tf_op jit(solution)/shard_map/all_to_all | solution.py:30
  219.5 1.4 convert_bitcast_fusion
  220.9 0.0 copy-start.1
  220.9 1.1 copy.22
  222.0 0.8 copy-done.1
  222.8 8.3 %fusion.38 = (f32[8,1024]{1,0:T(8,128)S(1)}, f32[8,192,1024]{2,1,0:T(8,128)}) fusion(f32[192,8,1024]{2,1,0:T(8,128)S(1)} %bitcast.46, bf16[8,192,1024]{2,1,0:T(8,128)(2,1)S(1)} %copy-done.1), kind=kLoop, calls=%fused_computation.40 | loop fusion | flops 11001856 | bytes 15761408 | tf_op jit(solution)/shard_map/reduce_sum | solution.py:12
  231.0 0.0 copy-start.3
  231.0 0.0 copy-start.4
  231.1 13.9 %psum.14 = f32[8,1024]{1,0:T(8,128)S(1)} all-reduce(f32[8,1024]{1,0:T(8,128)S(1)} %get-tuple-element.5), channel_id=1, replica_groups=mesh['seq'=64,'chan'=4] {'chan'}, use_global_device_ids=true, to_apply=%region_1.0 | all-reduce | flops 8192 | bytes 65536 | tf_op jit(solution)/shard_map/psum | solution.py:12
  245.0 3.7 %multiply_reduce_fusion = f32[8,1024]{1,0:T(8,128)S(1)} fusion(f32[8,192,1024]{2,1,0:T(8,128)} %get-tuple-element.6, f32[8,1024]{1,0:T(8,128)S(1)} %broadcast_multiply_fusion), kind=kLoop, calls=%fused_computation.21 | loop fusion | flops 4710400 | bytes 6356992 | tf_op jit(solution)/shard_map/reduce_sum | solution.py:15
  248.6 12.5 %psum.15 = f32[8,1024]{1,0:T(8,128)S(1)} all-reduce(f32[8,1024]{1,0:T(8,128)S(1)} %multiply_reduce_fusion), channel_id=1, replica_groups=mesh['seq'=64,'chan'=4] {'chan'}, use_global_device_ids=true, to_apply=%region_3.0 | all-reduce | flops 8192 | bytes 65536 | tf_op jit(solution)/shard_map/psum | solution.py:15
  261.2 0.0 copy-done.3
  261.2 0.0 copy-done.4
  261.2 14.8 %fusion.16 = bf16[8,192,1024]{2,1,0:T(8,128)(2,1)} fusion(f32[8,192,1024]{2,1,0:T(8,128)} %get-tuple-element.6, f32[8,1024]{1,0:T(8,128)S(1)} %add_rsqrt_fusion, f32[8,1024]{1,0:T(8,128)S(1)} %broadcast_multiply_fusion, bf16[1,192,768]{2,1,0:T(8,128)(2,1)S(1)} %copy-done.3, bf16[1,192,768]{2,1,0:T(8,128)(2,1)S(1)} %copy-done.4), kind=kOutput, calls=%fused_computation.19 | convolution fusion | flops 4896325632 | bytes 10092544 | tf_op jit(solution)/shard_map/xhy,kh->xky/dot_general | solution.py:20
  (2 shorter events, 0.0 us)
Async XLA Ops:
  0.0 1.6 copy-start
  7.7 95.0 %copy-start.2 = (bf16[512,512]{1,0:T(8,128)(2,1)S(1)}, bf16[512,512]{1,0:T(8,128)(2,1)}, u32[]{:S(2)}) copy-start(bf16[512,512]{1,0:T(8,128)(2,1)} %param.9) | copy-start | bytes 1572868
  220.9 1.9 copy-start.1
  231.0 30.1 %copy-start.3 = (bf16[1,192,768]{2,1,0:T(8,128)(2,1)S(1)}, bf16[1,192,768]{2,1,0:T(8,128)(2,1)}, u32[]{:S(2)}) copy-start(bf16[1,192,768]{2,1,0:T(8,128)(2,1)} %param.11) | copy-start | bytes 884740
  231.0 30.1 %copy-start.4 = (bf16[1,192,768]{2,1,0:T(8,128)(2,1)S(1)}, bf16[1,192,768]{2,1,0:T(8,128)(2,1)}, u32[]{:S(2)}) copy-start(bf16[1,192,768]{2,1,0:T(8,128)(2,1)} %param.10) | copy-start | bytes 884740

commit v2 on v1

v2 whole, which is shorter than its diff:
```python
import jax
import jax.numpy as jnp
from jax import lax
from jax.experimental import pallas as pl
from jax.experimental.pallas import tpu as pltpu
from jax.sharding import PartitionSpec as P

ROWS = 8
CH = 192
COLS = 1024
HID = 768
D = 768
PEERS = 64
PARTS = 4
W = 128
NCH = COLS // W
OWN = CH // PEERS
GA = ROWS * PEERS
MESH = pl.DeviceIdType.MESH
F32 = jnp.float32
BF16 = jnp.bfloat16


def peer(me, i):
    y, x, z, c = me // 16, (me // 4) % 4, (me // 2) % 2, me % 2
    y = (y + i // 16) % 4
    x = (x + (i // 4) % 4) % 4
    z = (z + (i // 2) % 2) % 2
    c = (c + i % 2) % 2
    return ((y * 4 + x) * 2 + z) * 2 + c


def loop(lo, hi, f):
    def step(i, carry):
        f(i)
        return carry

    lax.fori_loop(lo, hi, step, 0)


def layer_kernel(
    tok_hbm, gain_hbm, rf_hbm, cf_hbm, up_hbm, down_hbm, out_hbm,
    tok, gain, rf, cf, up, down, filt, recv, mix, back, gated, stat, result,
    in_sem, rf_sem, gain_sem, fs_sem, fr_sem, bs_sem, br_sem, ss_sem, sr_sem, out_sem,
):
    me = lax.axis_index("seq")
    part = lax.axis_index("chan")

    def cols(j):
        return pl.ds(pl.multiple_of(j * W, W), W)

    def rf_copy(j):
        return pltpu.make_async_copy(rf_hbm.at[cols(j)], rf.at[cols(j)], rf_sem.at[j])

    def gain_copy(j):
        return pltpu.make_async_copy(gain_hbm.at[:, :, cols(j)], gain.at[j], gain_sem.at[j])

    tok_copy = pltpu.make_async_copy(tok_hbm, tok, in_sem.at[0])
    weights = [
        pltpu.make_async_copy(cf_hbm, cf, in_sem.at[1]),
        pltpu.make_async_copy(up_hbm, up, in_sem.at[2]),
        pltpu.make_async_copy(down_hbm, down, in_sem.at[3]),
    ]
    tok_copy.start()

    def start_chunk(j):
        rf_copy(j).start()
        gain_copy(j).start()

    loop(0, NCH, start_chunk)
    for copy in weights:
        copy.start()

    barrier = pltpu.get_barrier_semaphore()

    def greet(i):
        pl.semaphore_signal(barrier, inc=1, device_id=(peer(me, i), part), device_id_type=MESH)

    loop(1, PEERS, greet)
    for i in range(1, PARTS):
        pl.semaphore_signal(barrier, inc=1, device_id=(me, (part + i) % PARTS), device_id_type=MESH)

    i0 = lax.broadcasted_iota(jnp.int32, (128, 128), 0)
    i1 = lax.broadcasted_iota(jnp.int32, (128, 128), 1)
    to_chan = jnp.where(i1 == (i0 % 8) * 16 + i0 // 8, 1.0, 0.0).astype(BF16)
    to_rows = jnp.where(i1 == (i0 % 16) * 8 + i0 // 16, 1.0, 0.0).astype(BF16)
    filt_rows = filt.reshape(NCH * CH * ROWS, W)
    back_rows = back.reshape(NCH * CH * ROWS, W)

    def block(j, c):
        return pl.ds(pl.multiple_of(j * (CH * ROWS) + c * ROWS, 128), 128)

    def row_mix(j):
        rf_copy(j).wait()
        gain_copy(j).wait()
        for c0 in range(0, CH, 64):
            lhs = tok[:, c0 : c0 + 64, :].reshape(ROWS * 64, COLS)
            spun = lax.dot_general(lhs, rf[cols(j), :], (((1,), (1,)), ((), ())), preferred_element_type=F32)
            spun = spun.reshape(ROWS, 64, W)
            own = (gain[j, :, c0 : c0 + 64, :].astype(F32) * spun).astype(BF16)
            for c in range(0, 64, 16):
                piece = own[:, c : c + 16, :].reshape(128, W)
                filt_rows[block(j, c0 + c), :] = jnp.dot(to_chan, piece, preferred_element_type=F32).astype(BF16)

    def my_rows(d):
        return pl.ds(pl.multiple_of(d * ROWS, ROWS), ROWS)

    def send_filtered(j):
        def one(i):
            d = peer(me, i)
            pltpu.make_async_remote_copy(
                src_ref=filt.at[j, pl.ds(OWN * d, OWN)],
                dst_ref=recv.at[j, :, my_rows(me), :],
                send_sem=fs_sem.at[j],
                recv_sem=fr_sem.at[j],
                device_id=(d, part),
                device_id_type=MESH,
            ).start()

        loop(1, PEERS, one)
        pltpu.make_async_copy(filt.at[j, pl.ds(OWN * me, OWN)], recv.at[j, :, my_rows(me), :], fr_sem.at[j]).start()

    def col_mix(j):
        pltpu.make_async_copy(recv.at[j], recv.at[j], fr_sem.at[j]).wait()
        rhs = jnp.concatenate([recv[j, c] for c in range(OWN)], axis=1)
        mixed = jnp.dot(cf[...], rhs, preferred_element_type=F32).astype(BF16)
        for c in range(OWN):
            mix[j, c] = mixed[:, c * W : (c + 1) * W]

    def send_mixed(j):
        def one(i):
            d = peer(me, i)
            pltpu.make_async_remote_copy(
                src_ref=mix.at[j, :, my_rows(d), :],
                dst_ref=back.at[j, pl.ds(OWN * me, OWN)],
                send_sem=bs_sem.at[j],
                recv_sem=br_sem.at[j],
                device_id=(d, part),
                device_id_type=MESH,
            ).start()

        loop(1, PEERS, one)
        pltpu.make_async_copy(mix.at[j, :, my_rows(me), :], back.at[j, pl.ds(OWN * me, OWN)], br_sem.at[j]).start()

    def gate(j):
        pltpu.make_async_copy(back.at[j], back.at[j], br_sem.at[j]).wait()
        slot = j % 2
        total = jnp.zeros((ROWS, W), F32)
        for c in range(0, CH, 16):
            mixed = jnp.dot(to_rows, back_rows[block(j, c), :], preferred_element_type=F32).reshape(ROWS, 16, W)
            src = tok[:, c : c + 16, cols(j)].astype(F32)
            value = src + mixed * jax.nn.sigmoid(src)
            gated[slot, :, c : c + 16, :] = value
            total = total + jnp.sum(value, axis=1)
        mean = total * (1.0 / CH)
        squares = jnp.zeros((ROWS, W), F32)
        for c in range(0, CH, 16):
            off = gated[slot, :, c : c + 16, :] - mean[:, None, :]
            squares = squares + jnp.sum(off * off, axis=1)
        stat[j, part, 0] = total
        stat[j, part, 1] = squares
        for i in range(1, PARTS):
            pltpu.make_async_remote_copy(
                src_ref=stat.at[j, part],
                dst_ref=stat.at[j, part],
                send_sem=ss_sem.at[j],
                recv_sem=sr_sem.at[j],
                device_id=(me, (part + i) % PARTS),
                device_id_type=MESH,
            ).start()

    def out_copy(j):
        return pltpu.make_async_copy(result.at[j], out_hbm.at[:, :, cols(j)], out_sem.at[j])

    def channel_mlp(j):
        three = stat.at[j, pl.ds(0, PARTS - 1)]
        pltpu.make_async_copy(three, three, sr_sem.at[j]).wait()
        slot = j % 2
        totals = [stat[j, p, 0] for p in range(PARTS)]
        mean = (totals[0] + totals[1] + totals[2] + totals[3]) * (1.0 / D)
        spread = jnp.zeros((ROWS, W), F32)
        for p in range(PARTS):
            off = totals[p] * (1.0 / CH) - mean
            spread = spread + (stat[j, p, 1] + CH * (off * off))
        scale = lax.rsqrt(spread * (1.0 / D) + 1e-05)
        for r0 in range(0, ROWS, 2):
            value = jnp.concatenate([gated[slot, r] for r in (r0, r0 + 1)], axis=1)
            m = jnp.concatenate([mean[r : r + 1] for r in (r0, r0 + 1)], axis=1)
            s = jnp.concatenate([scale[r : r + 1] for r in (r0, r0 + 1)], axis=1)
            normed = ((value - m) * s).astype(BF16)
            hidden = jax.nn.gelu(jnp.dot(up[...], normed, preferred_element_type=F32)).astype(BF16)
            final = (value + jnp.dot(down[...], hidden, preferred_element_type=F32)).astype(BF16)
            result[j, r0] = final[:, :W]
            result[j, r0 + 1] = final[:, W:]
        out_copy(j).start()

    tok_copy.wait()

    def first(j):
        row_mix(j)

        @pl.when(j == 0)
        def _():
            pl.semaphore_wait(barrier, PEERS - 1 + PARTS - 1)

        send_filtered(j)

    loop(0, NCH, first)
    for copy in weights:
        copy.wait()

    def second(j):
        col_mix(j)
        send_mixed(j)

    loop(0, NCH, second)
    gate(0)

    def third(j):
        gate(j)
        channel_mlp(j - 1)

    loop(1, NCH, third)
    channel_mlp(NCH - 1)

    def drain(j):
        rest = filt.at[j, pl.ds(0, CH - OWN)]
        pltpu.make_async_copy(rest, rest, fs_sem.at[j]).wait()
        pltpu.make_async_copy(rest, rest, bs_sem.at[j]).wait()
        three = stat.at[j, pl.ds(0, PARTS - 1)]
        pltpu.make_async_copy(three, three, ss_sem.at[j]).wait()
        out_copy(j).wait()

    loop(0, NCH, drain)


def body(tokens, filter_gain, row_factor, col_factor, up_weight, down_weight):
    dma = pltpu.SemaphoreType.DMA
    return pl.pallas_call(
        layer_kernel,
        name="mixer_layer",
        out_shape=jax.ShapeDtypeStruct((ROWS, CH, COLS), BF16),
        in_specs=[pl.BlockSpec(memory_space=pl.ANY)] * 6,
        out_specs=pl.BlockSpec(memory_space=pl.ANY),
        scratch_shapes=[
            pltpu.VMEM((ROWS, CH, COLS), BF16),
            pltpu.VMEM((NCH, ROWS, CH, W), BF16),
            pltpu.VMEM((COLS, COLS), BF16),
            pltpu.VMEM((GA, GA), BF16),
            pltpu.VMEM((HID, CH), BF16),
            pltpu.VMEM((CH, HID), BF16),
            pltpu.VMEM((NCH, CH, ROWS, W), BF16),
            pltpu.VMEM((NCH, OWN, GA, W), BF16),
            pltpu.VMEM((NCH, OWN, GA, W), BF16),
            pltpu.VMEM((NCH, CH, ROWS, W), BF16),
            pltpu.VMEM((2, ROWS, CH, W), F32),
            pltpu.VMEM((NCH, PARTS, 2, ROWS, W), F32),
            pltpu.VMEM((NCH, ROWS, CH, W), BF16),
            dma((4,)),
        ]
        + [dma((NCH,))] * 9,
        compiler_params=pltpu.CompilerParams(
            collective_id=0, has_side_effects=True, vmem_limit_bytes=60 * 2**20
        ),
    )(tokens, filter_gain, row_factor, col_factor, up_weight[0].T, down_weight[0])


def solution(mesh):
    return jax.shard_map(
        body,
        mesh=mesh,
        in_specs=(
            P("seq", "chan", None),
            P("seq", "chan", None),
            P(),
            P(),
            P("chan", None, None),
            P("chan", None, None),
        ),
        out_specs=P("seq", "chan", None),
        check_vma=False,
    )
```

time: 281 us -> 183 us (0.65); the launches traced: 276 us -> 181 us
  blocking collectives: 225 us -> 0 us
  Pallas kernels: 0 us -> 176 us
  matrix products: 24.4 us -> 0 us
  other arithmetic: 13.3 us -> 0 us
  local copies, waits for them, and re-layouts: 13 us -> 5.74 us
    all_to_all x2 -> x0, blocking collectives: 199 us -> none  [the longest x1 106 us: body(): lax.all_to_all(mixed.astype(jnp.bfloat16), 'seq', split_axis=1, concat_ax...]
    pallas_call x0 -> x1, Pallas kernels: none -> 176 us  [body(): pl.pallas_call(layer_kernel, name='mixer_layer', out_shape=jax.ShapeDtype...]
    psum x2 -> x0, blocking collectives: 26.4 us -> none  [the longest x1 13.9 us: finish(): total = lax.psum(jnp.sum(gated, axis=1), 'chan')]
    dot_general x3 -> x0, matrix products: 24.4 us -> none  [the longest x1 14.8 us: finish(): jnp.einsum('xhy,kh->xky', hidden, down_weight[0], preferred_element_type=...]
    reduce_sum x2 -> x0, other arithmetic: 11.9 us -> none  [the longest x1 8.29 us: finish(): total = lax.psum(jnp.sum(gated, axis=1), 'chan')]
    convert_element_type x2 -> x0, local copies, waits for them, and re-layouts: 8.89 us -> none  [the longest x1 7.78 us: body(): mixed.astype(jnp.bfloat16)]
    unnamed x10 -> x2, local copies, waits for them, and re-layouts: 2.37 us -> 5.74 us
where the time goes in v2:
time: 183 us; the launch traced here: 181 us
  Pallas kernels  176 us (96%)
  local copies, waits for them, and re-layouts  5.74 us (3%)
    pallas_call x1, Pallas kernels, body(): pl.pallas_call(layer_kernel, name='mixer_layer', out_shape=jax.ShapeDtype...  176 us
    unnamed x2, local copies, waits for them, and re-layouts  5.74 us

profile of v2, /device:TPU:1, one launch (start us, length us, event | category | flops | bytes accessed | tf_op | source)
XLA Modules:
  0.0 181.3 jit_solution(15228547119248198219)
XLA Ops:
  0.0 1.9 %copy.7 = bf16[1,192,768]{1,2,0:T(8,128)(2,1)} copy(bf16[1,192,768]{2,1,0:T(8,128)(2,1)} %param.10) | data formatting | bytes 589824 | tf_op args[4]
  1.9 175.5 %mixer_layer.1 = bf16[8,192,1024]{2,1,0:T(8,128)(2,1)} custom-call(bf16[8,192,1024]{2,1,0:T(8,128)(2,1)} %tok_hbm.1, bf16[8,192,1024]{2,1,0:T(8,128)(2,1)} %gain_hbm.1, bf16[1024,1024]{1,0:T(8,128)(2,1)} %rf_hbm.1, bf16[512,512]{1,0:T(8,128)(2,1)} %cf_hbm.1, bf16[768,192]{1,0:T(8,128)(2,1)} %bitcast.4, bf16[192,768]{1,0:T(8,128)(2,1)} %bitcast.5), custom_call_target="tpu_custom_call" | custom-call | tf_op jit(solution)/shard_map/mixer_layer/pallas_call | solution.py:239
  177.4 3.9 %copy.9 = bf16[8,192,1024]{2,1,0:T(8,128)(2,1)} copy(bf16[8,192,1024]{2,1,0:T(8,128)(2,1)} %mixer_layer.1) | data formatting | bytes 6291456

commit v3 on v2

--- a/solution.py
+++ b/solution.py
@@ -15,6 +15,9 @@
 W = 128
 NCH = COLS // W
 OWN = CH // PEERS
+PLANES = 4
+PLANE = PEERS // PLANES
+PCH = PLANE * OWN
 GA = ROWS * PEERS
 MESH = pl.DeviceIdType.MESH
 F32 = jnp.float32
@@ -40,7 +43,7 @@
 
 def layer_kernel(
     tok_hbm, gain_hbm, rf_hbm, cf_hbm, up_hbm, down_hbm, out_hbm,
-    tok, gain, rf, cf, up, down, filt, recv, mix, back, gated, stat, result,
+    tok, gain, rf, cf, up, down, up_t, filt, recv, mix, back, gated, stat, result,
     in_sem, rf_sem, gain_sem, fs_sem, fr_sem, bs_sem, br_sem, ss_sem, sr_sem, out_sem,
 ):
     me = lax.axis_index("seq")
@@ -55,21 +58,21 @@
     def gain_copy(j):
         return pltpu.make_async_copy(gain_hbm.at[:, :, cols(j)], gain.at[j], gain_sem.at[j])
 
-    tok_copy = pltpu.make_async_copy(tok_hbm, tok, in_sem.at[0])
+    def tok_copy(r):
+        return pltpu.make_async_copy(tok_hbm.at[r], tok.at[r], in_sem.at[0])
+
     weights = [
         pltpu.make_async_copy(cf_hbm, cf, in_sem.at[1]),
         pltpu.make_async_copy(up_hbm, up, in_sem.at[2]),
         pltpu.make_async_copy(down_hbm, down, in_sem.at[3]),
     ]
-    tok_copy.start()
+    loop(0, ROWS, lambda r: tok_copy(r).start())
 
     def start_chunk(j):
         rf_copy(j).start()
         gain_copy(j).start()
 
-    loop(0, NCH, start_chunk)
-    for copy in weights:
-        copy.start()
+    start_chunk(0)
 
     barrier = pltpu.get_barrier_semaphore()
 
@@ -90,22 +93,20 @@
     def block(j, c):
         return pl.ds(pl.multiple_of(j * (CH * ROWS) + c * ROWS, 128), 128)
 
-    def row_mix(j):
-        rf_copy(j).wait()
-        gain_copy(j).wait()
-        for c0 in range(0, CH, 64):
-            lhs = tok[:, c0 : c0 + 64, :].reshape(ROWS * 64, COLS)
-            spun = lax.dot_general(lhs, rf[cols(j), :], (((1,), (1,)), ((), ())), preferred_element_type=F32)
-            spun = spun.reshape(ROWS, 64, W)
-            own = (gain[j, :, c0 : c0 + 64, :].astype(F32) * spun).astype(BF16)
-            for c in range(0, 64, 16):
-                piece = own[:, c : c + 16, :].reshape(128, W)
-                filt_rows[block(j, c0 + c), :] = jnp.dot(to_chan, piece, preferred_element_type=F32).astype(BF16)
+    def row_mix(j, plane):
+        c0 = pl.multiple_of(plane * PCH, 16)
+        lhs = tok[:, pl.ds(c0, PCH), :].reshape(ROWS * PCH, COLS)
+        spun = lax.dot_general(lhs, rf[cols(j), :], (((1,), (1,)), ((), ())), preferred_element_type=F32)
+        spun = spun.reshape(ROWS, PCH, W)
+        own = (gain[j, :, pl.ds(c0, PCH), :].astype(F32) * spun).astype(BF16)
+        for c in range(0, PCH, 16):
+            piece = own[:, c : c + 16, :].reshape(128, W)
+            filt_rows[block(j, c0 + c), :] = jnp.dot(to_chan, piece, preferred_element_type=F32).astype(BF16)
 
     def my_rows(d):
         return pl.ds(pl.multiple_of(d * ROWS, ROWS), ROWS)
 
-    def send_filtered(j):
+    def send_filtered(j, lo, hi):
         def one(i):
             d = peer(me, i)
             pltpu.make_async_remote_copy(
@@ -117,7 +118,9 @@
                 device_id_type=MESH,
             ).start()
 
-        loop(1, PEERS, one)
+        loop(lo, hi, one)
+
+    def keep_filtered(j):
         pltpu.make_async_copy(filt.at[j, pl.ds(OWN * me, OWN)], recv.at[j, :, my_rows(me), :], fr_sem.at[j]).start()
 
     def col_mix(j):
@@ -188,26 +191,42 @@
             m = jnp.concatenate([mean[r : r + 1] for r in (r0, r0 + 1)], axis=1)
             s = jnp.concatenate([scale[r : r + 1] for r in (r0, r0 + 1)], axis=1)
             normed = ((value - m) * s).astype(BF16)
-            hidden = jax.nn.gelu(jnp.dot(up[...], normed, preferred_element_type=F32)).astype(BF16)
+            hidden = jax.nn.gelu(jnp.dot(up_t[...], normed, preferred_element_type=F32)).astype(BF16)
             final = (value + jnp.dot(down[...], hidden, preferred_element_type=F32)).astype(BF16)
             result[j, r0] = final[:, :W]
             result[j, r0 + 1] = final[:, W:]
         out_copy(j).start()
 
-    tok_copy.wait()
+    pltpu.make_async_copy(tok_hbm, tok, in_sem.at[0]).wait()
+
+    def plane_of(step):
+        return (me // PLANE + step) % PLANES
 
     def first(j):
-        row_mix(j)
+        rf_copy(j).wait()
+        gain_copy(j).wait()
+        row_mix(j, plane_of(0))
 
         @pl.when(j == 0)
         def _():
             pl.semaphore_wait(barrier, PEERS - 1 + PARTS - 1)
-
-        send_filtered(j)
+            loop(1, NCH, start_chunk)
+            for copy in weights:
+                copy.start()
+
+        send_filtered(j, 1, PLANE)
+        keep_filtered(j)
+
+        def later(step):
+            row_mix(j, plane_of(step))
+            send_filtered(j, step * PLANE, step * PLANE + PLANE)
+
+        loop(1, PLANES, later)
 
     loop(0, NCH, first)
     for copy in weights:
         copy.wait()
+    up_t[...] = up[...].astype(F32).T.astype(BF16)
 
     def second(j):
         col_mix(j)
@@ -247,8 +266,9 @@
             pltpu.VMEM((NCH, ROWS, CH, W), BF16),
             pltpu.VMEM((COLS, COLS), BF16),
             pltpu.VMEM((GA, GA), BF16),
+            pltpu.VMEM((CH, HID), BF16),
+            pltpu.VMEM((CH, HID), BF16),
             pltpu.VMEM((HID, CH), BF16),
-            pltpu.VMEM((CH, HID), BF16),
             pltpu.VMEM((NCH, CH, ROWS, W), BF16),
             pltpu.VMEM((NCH, OWN, GA, W), BF16),
             pltpu.VMEM((NCH, OWN, GA, W), BF16),
@@ -262,7 +282,7 @@
         compiler_params=pltpu.CompilerParams(
             collective_id=0, has_side_effects=True, vmem_limit_bytes=60 * 2**20
         ),
-    )(tokens, filter_gain, row_factor, col_factor, up_weight[0].T, down_weight[0])
+    )(tokens, filter_gain, row_factor, col_factor, up_weight[0], down_weight[0])
 
 
 def solution(mesh):

time: 183 us -> 180 us (0.984)
  local copies, waits for them, and re-layouts: 5.74 us -> 3.86 us
    unnamed x2 -> x1, local copies, waits for them, and re-layouts: 5.74 us -> 3.86 us
where the time goes in v3:
time: 180 us; the launch traced here: 179 us
  Pallas kernels  175 us (97%)
  local copies, waits for them, and re-layouts  3.86 us (2%)
    pallas_call x1, Pallas kernels, body(): pl.pallas_call(layer_kernel, name='mixer_layer', out_shape=jax.ShapeDtype...  175 us
    unnamed x1, local copies, waits for them, and re-layouts  3.86 us

profile of v3, /device:TPU:1, one launch (start us, length us, event | category | flops | bytes accessed | tf_op | source)
XLA Modules:
  0.0 178.9 jit_solution(3953386588424973084)
XLA Ops:
  0.0 175.0 %mixer_layer.1 = bf16[8,192,1024]{2,1,0:T(8,128)(2,1)} custom-call(bf16[8,192,1024]{2,1,0:T(8,128)(2,1)} %tok_hbm.1, bf16[8,192,1024]{2,1,0:T(8,128)(2,1)} %gain_hbm.1, bf16[1024,1024]{1,0:T(8,128)(2,1)} %rf_hbm.1, bf16[512,512]{1,0:T(8,128)(2,1)} %cf_hbm.1, bf16[192,768]{1,0:T(8,128)(2,1)} %bitcast.2, bf16[192,768]{1,0:T(8,128)(2,1)} %bitcast.3), custom_call_target="tpu_custom_call" | custom-call | tf_op jit(solution)/shard_map/mixer_layer/pallas_call | solution.py:258
  175.0 3.9 %copy.8 = bf16[8,192,1024]{2,1,0:T(8,128)(2,1)} copy(bf16[8,192,1024]{2,1,0:T(8,128)(2,1)} %mixer_layer.1) | data formatting | bytes 6291456

commit v4 on v3

--- a/solution.py
+++ b/solution.py
@@ -19,6 +19,7 @@
 PLANE = PEERS // PLANES
 PCH = PLANE * OWN
 GA = ROWS * PEERS
+LAG = 3
 MESH = pl.DeviceIdType.MESH
 F32 = jnp.float32
 BF16 = jnp.bfloat16
@@ -229,18 +230,20 @@
     up_t[...] = up[...].astype(F32).T.astype(BF16)
 
     def second(j):
-        col_mix(j)
-        send_mixed(j)
-
-    loop(0, NCH, second)
-    gate(0)
-
-    def third(j):
-        gate(j)
-        channel_mlp(j - 1)
-
-    loop(1, NCH, third)
-    channel_mlp(NCH - 1)
+        @pl.when(j < NCH)
+        def _():
+            col_mix(j)
+            send_mixed(j)
+
+        @pl.when(jnp.logical_and(j >= LAG, j < NCH + LAG))
+        def _():
+            gate(j - LAG)
+
+        @pl.when(j > LAG)
+        def _():
+            channel_mlp(j - LAG - 1)
+
+    loop(0, NCH + LAG + 1, second)
 
     def drain(j):
         rest = filt.at[j, pl.ds(0, CH - OWN)]

time: 180 us -> 184 us (1.022)
  Pallas kernels: 175 us -> 180 us
    pallas_call x1, Pallas kernels: 175 us -> 180 us  [body(): pl.pallas_call(layer_kernel, name='mixer_layer', out_shape=jax.ShapeDtype...]
where the time goes in v4:
time: 184 us
  Pallas kernels  180 us (98%)
  local copies, waits for them, and re-layouts  3.86 us (2%)
    pallas_call x1, Pallas kernels, body(): pl.pallas_call(layer_kernel, name='mixer_layer', out_shape=jax.ShapeDtype...  180 us
    unnamed x1, local copies, waits for them, and re-layouts  3.86 us

profile of v4, /device:TPU:1, one launch (start us, length us, event | category | flops | bytes accessed | tf_op | source)
XLA Modules:
  0.0 183.8 jit_solution(18356292953330433622)
XLA Ops:
  0.0 179.9 %mixer_layer.1 = bf16[8,192,1024]{2,1,0:T(8,128)(2,1)} custom-call(bf16[8,192,1024]{2,1,0:T(8,128)(2,1)} %tok_hbm.1, bf16[8,192,1024]{2,1,0:T(8,128)(2,1)} %gain_hbm.1, bf16[1024,1024]{1,0:T(8,128)(2,1)} %rf_hbm.1, bf16[512,512]{1,0:T(8,128)(2,1)} %cf_hbm.1, bf16[192,768]{1,0:T(8,128)(2,1)} %bitcast.2, bf16[192,768]{1,0:T(8,128)(2,1)} %bitcast.3), custom_call_target="tpu_custom_call" | custom-call | tf_op jit(solution)/shard_map/mixer_layer/pallas_call | solution.py:261
  179.9 3.9 %copy.8 = bf16[8,192,1024]{2,1,0:T(8,128)(2,1)} copy(bf16[8,192,1024]{2,1,0:T(8,128)(2,1)} %mixer_layer.1) | data formatting | bytes 6291456
